TPU v7x, 256 devices: a whole 4x4x8 slice. The times are simulated.
256 devices in a mesh: dom: 32 (over z, x), rep: 8 (over y, core).
Axes of the slice: x: 4, y: 4, z: 8, core: 2. Of those that a mesh axis runs over, the one named last changes fastest.
Arguments:
- grad_out: bfloat16 [262144, 512], P(('dom', 'rep')), may hold values from -6 to 6
- features: bfloat16 [262144, 512], P(('dom', 'rep')), may hold values from -24 to 24
- weight: bfloat16 [512, 512], replicated, may hold values from -0.25 to 0.25
- edge_blocks: bfloat16 [32768, 128, 128], P(('dom', 'rep')), may hold values from -0.25 to 0.25
- block_index: int32 [32768, 2], P(('dom', 'rep')), may hold values from 0 to 63, as said below
- block_count: int32 [256], P(('dom', 'rep')), may hold values from 25 to 128, as said below
- node_perm: int32 [262144], P(('dom', 'rep')), may hold values from 0 to 262143, as said below
Outputs:
- grad_input: bfloat16 [262144, 512], P(('dom', 'rep'))
- weight_grad: float32 [512, 512], P('dom', 'rep')
Inputs may be any that keep to these rules, and one draw needn't show every extreme that they name: A node at input row i, held by device s = i // 1024, lands at node_perm[i] = t * 1024 + s * 4 + k with 0 <= k < 4; each device's rows cover every pair (t, k) exactly once, so every device passes exactly 4 rows to every device. `block_index`: first column below 64, second below 8; blocks may repeat. `block_count`: in each group of 8 devices along rep exactly one device has 128 live slots; the others have between 25 and 64.
All inputs are finite; a program needn't handle non-finite values.
Results may differ from a plain program's by a relative error of at most 0.005.
Values may be sent and summed in bfloat16 or wider, within the bound.
A program may use at most 64 MiB of HBM per device.

v0:
```python
import math
import jax
import jax.numpy as jnp
from jax import lax
from jax.sharding import PartitionSpec as P


def cut_along(x, dim, length):
    before, after = (x.shape[:dim], x.shape[dim + 1 :])
    return jnp.moveaxis(x.reshape(*before, length, -1, *after), dim, 0)


def in_order(parts, dim):
    parts = jnp.moveaxis(parts, 0, dim)
    shape = parts.shape
    return parts.reshape(*shape[:dim], shape[dim] * shape[dim + 1], *shape[dim + 2 :])


def one_exchange(x, axis, axes, splits, concats):
    sizes = [lax.axis_size(a) for a in axes]
    parts = cut_along(x, splits[0], sizes[0])
    parts = jnp.moveaxis(cut_along(parts, splits[1] + 1, sizes[1]), 0, 1)
    inside = parts.shape[2:]
    parts = parts.reshape(-1, *inside)
    parts = lax.all_to_all(parts, axis, split_axis=0, concat_axis=0, tiled=True)
    parts = in_order(parts.reshape(*sizes, *inside), concats[0] + 1)
    return in_order(parts, concats[1])


def sent_and_summed(x, axis, dim):
    parts = cut_along(x, dim, lax.axis_size(axis))
    arrived = lax.all_to_all(parts, axis, split_axis=0, concat_axis=0, tiled=True)
    return arrived.sum(axis=0)


def accumulate(running, block_values, index_values, live_count, stacked):
    group_len = 16
    turn_count = (live_count + group_len - 1) // group_len

    def add_group(turn_index, current):
        first_slot = turn_index * group_len
        block_part = lax.dynamic_slice_in_dim(block_values, first_slot, group_len, 0)
        index_part = lax.dynamic_slice_in_dim(index_values, first_slot, group_len, 0)
        alive_mask = first_slot + jnp.arange(group_len) < live_count
        source = jnp.take(stacked, index_part[:, 0], axis=0)
        products = jnp.einsum(
            "kij,kif->kjf", block_part, source, preferred_element_type=jnp.float32
        )
        targets = index_part[:, 1]
        onehot = jnp.where(
            alive_mask[:, None] & (targets[:, None] == jnp.arange(current.shape[0])[None, :]),
            1.0,
            0.0,
        ).astype(jnp.float32)
        return current + jnp.einsum(
            "kc,kjf->cjf",
            onehot,
            products,
            precision=lax.Precision.HIGHEST,
            preferred_element_type=jnp.float32,
        )

    return lax.fori_loop(0, turn_count, add_group, running)


def on_device(grad_out, features, weight, edge_blocks, block_index, block_count, node_perm):
    dom_count = lax.axis_size("dom")
    rep_count = lax.axis_size("rep")
    device_count = dom_count * rep_count
    row_count = grad_out.shape[0]
    feat_width = grad_out.shape[1]
    slot_rows = row_count // device_count
    block_side = edge_blocks.shape[1]
    col_blocks = row_count // block_side
    target_device = node_perm // row_count
    within_slot = node_perm % slot_rows
    target_slot = target_device * slot_rows + within_slot
    ordered = jnp.zeros_like(grad_out).at[target_slot].set(grad_out)
    ordered = ordered.reshape(dom_count, rep_count, slot_rows, feat_width)
    arrived = one_exchange(ordered, ("dom", "rep"), ("dom", "rep"), (0, 1), (0, 1))
    local_rows = arrived.reshape(row_count, feat_width)
    whole = lax.all_gather(local_rows, "rep", axis=0, tiled=True)
    stacked = whole.reshape(-1, block_side, feat_width)
    running = jnp.zeros((col_blocks, block_side, feat_width), jnp.float32)
    running = accumulate(running, edge_blocks, block_index, block_count[0], stacked)
    aggregated = running.reshape(row_count, feat_width).astype(jnp.bfloat16)
    grad_input = lax.dot_general(
        aggregated, weight, (((1,), (1,)), ((), ())), preferred_element_type=jnp.float32
    ).astype(jnp.bfloat16)
    scale_factor = 1.0 / math.sqrt(row_count * device_count)
    partial_rows = sent_and_summed(
        lax.dot_general(
            features, aggregated, (((0,), (0,)), ((), ())), preferred_element_type=jnp.float32
        )
        * scale_factor,
        "dom",
        0,
    )
    weight_grad = sent_and_summed(partial_rows, "rep", 1)
    return (grad_input, weight_grad)


def solution(mesh):
    in_specs = (
        P(("dom", "rep"), None),
        P(("dom", "rep"), None),
        P(),
        P(("dom", "rep"), None, None),
        P(("dom", "rep"), None),
        P(("dom", "rep")),
        P(("dom", "rep")),
    )
    out_specs = (P(("dom", "rep"), None), P("dom", "rep"))
    return jax.shard_map(
        on_device, mesh=mesh, in_specs=in_specs, out_specs=out_specs, check_vma=False
    )
```

profile of v0, /device:TPU:1, one launch (start us, length us, event | category | flops | bytes accessed | tf_op | source)
XLA Modules:
  0.0 271.4 jit_solution(8153901035986305665)
XLA Ops:
  7.2 0.8 compare_select_fusion.1
  8.0 5.8 %scatter_custom_fusion = bf16[1024,512]{1,0:T(8,128)(2,1)S(1)} fusion(s32[1024]{0:T(1024)S(1)} %compare_select_fusion.1, bf16[1024,512]{1,0:T(8,128)(2,1)} %param.9, bf16[]{:T(256)} %constant.78.clone.1), kind=kCustom, calls=%fused_computation.32 | custom fusion | bytes 1049088 | tf_op jit(solution)/shard_map/scatter | solution.py:78
  14.1 45.9 %all_to_all.15 = bf16[256,1,1,4,512]{4,3,2,1,0:T(4,128)(2,1)S(1)} all-to-all(bf16[256,1,1,4,512]{4,3,2,1,0:T(4,128)(2,1)S(1)} %bitcast.38), channel_id=1, replica_groups=mesh['dom'=32,'rep'=8] {'dom','rep'}, dimensions={0} | all-to-all | bytes 2097152 | tf_op jit(solution)/shard_map/all_to_all | solution.py:25
  60.0 1.1 reshape_reshape.3
  61.8 46.9 %all-gather.2.cloned.1.call-done = bf16[8192,512]{1,0:T(8,128)(2,1)} async-done(((bf16[1024,512]{1,0:T(8,128)(2,1)}), bf16[8192,512]{1,0:T(8,128)(2,1)}) %all-gather.2.cloned.1.call-update) | async-done | bytes 8388624 | tf_op jit(solution)/shard_map/all_gather | solution.py:82
  108.7 1.7 broadcast_in_dim.29
  110.3 51.8 %while.10 = (s32[]{:T(128)}, f32[8,128,512]{2,0,1:T(8,128)}, s32[]{:T(128)}, s32[]{:T(128)}, s32[128,2]{0,1:T(2,128)S(1)}, /*index=5*/bf16[128,128,128]{2,1,0:T(...) while((s32[]{:T(128)}, f32[8,128,512]{2,0,1:T(8,128)}, ...), condition=%wide.region_2.3_spmd, body=%wide.region_1.2_spmd.sunk | while | flops 370673216 | bytes 19403756 | solution.py:63
  110.4 4.1 %gather_fusion = bf16[16,128,512]{2,1,0:T(8,128)(2,1)S(1)} fusion(bf16[64,128,512]{2,1,0:T(8,128)(2,1)} %get-tuple-element.147, s32[1024]{0:T(1024)S(1)} %pad_clamp_fusion.2), kind=kCustom, calls=%fused_computation.clone.1 | custom fusion | bytes 4194368 | tf_op jit(solution)/shard_map/while/body/jit(_take)/gather | solution.py:45
  114.5 1.8 fusion.44
  117.0 6.3 %fusion.45 = f32[8,128,512]{2,0,1:T(8,128)} fusion(f32[8,128,512]{2,0,1:T(8,128)} %get-tuple-element.131, f32[16,128,512]{2,1,0:T(8,128)S(1)} %fusion.44, s32[16]{0:T(128)S(1)} %get-tuple-element.118, pred[16]{0:T(512)(128)(4,1)S(1)} %add_compare_fusion.2), kind=kOutput, calls=%fused_computation.7.clone.1 | convolution fusion | flops 101187968 | bytes 8388688 | tf_op jit(solution)/shard_map/while/body/kc,kjf->cjf/dot_general | solution.py:55
  123.4 4.1 %gather_fusion = bf16[16,128,512]{2,1,0:T(8,128)(2,1)S(1)} fusion(bf16[64,128,512]{2,1,0:T(8,128)(2,1)} %get-tuple-element.147, s32[1024]{0:T(1024)S(1)} %pad_clamp_fusion.2), kind=kCustom, calls=%fused_computation.clone.1 | custom fusion | bytes 4194368 | tf_op jit(solution)/shard_map/while/body/jit(_take)/gather | solution.py:45
  127.4 1.8 fusion.44
  129.9 6.3 %fusion.45 = f32[8,128,512]{2,0,1:T(8,128)} fusion(f32[8,128,512]{2,0,1:T(8,128)} %get-tuple-element.131, f32[16,128,512]{2,1,0:T(8,128)S(1)} %fusion.44, s32[16]{0:T(128)S(1)} %get-tuple-element.118, pred[16]{0:T(512)(128)(4,1)S(1)} %add_compare_fusion.2), kind=kOutput, calls=%fused_computation.7.clone.1 | convolution fusion | flops 101187968 | bytes 8388688 | tf_op jit(solution)/shard_map/while/body/kc,kjf->cjf/dot_general | solution.py:55
  136.3 4.1 %gather_fusion = bf16[16,128,512]{2,1,0:T(8,128)(2,1)S(1)} fusion(bf16[64,128,512]{2,1,0:T(8,128)(2,1)} %get-tuple-element.147, s32[1024]{0:T(1024)S(1)} %pad_clamp_fusion.2), kind=kCustom, calls=%fused_computation.clone.1 | custom fusion | bytes 4194368 | tf_op jit(solution)/shard_map/while/body/jit(_take)/gather | solution.py:45
  140.4 1.8 fusion.44
  142.9 6.3 %fusion.45 = f32[8,128,512]{2,0,1:T(8,128)} fusion(f32[8,128,512]{2,0,1:T(8,128)} %get-tuple-element.131, f32[16,128,512]{2,1,0:T(8,128)S(1)} %fusion.44, s32[16]{0:T(128)S(1)} %get-tuple-element.118, pred[16]{0:T(512)(128)(4,1)S(1)} %add_compare_fusion.2), kind=kOutput, calls=%fused_computation.7.clone.1 | convolution fusion | flops 101187968 | bytes 8388688 | tf_op jit(solution)/shard_map/while/body/kc,kjf->cjf/dot_general | solution.py:55
  149.2 4.1 %gather_fusion = bf16[16,128,512]{2,1,0:T(8,128)(2,1)S(1)} fusion(bf16[64,128,512]{2,1,0:T(8,128)(2,1)} %get-tuple-element.147, s32[1024]{0:T(1024)S(1)} %pad_clamp_fusion.2), kind=kCustom, calls=%fused_computation.clone.1 | custom fusion | bytes 4194368 | tf_op jit(solution)/shard_map/while/body/jit(_take)/gather | solution.py:45
  153.3 1.8 fusion.44
  155.8 6.3 %fusion.45 = f32[8,128,512]{2,0,1:T(8,128)} fusion(f32[8,128,512]{2,0,1:T(8,128)} %get-tuple-element.131, f32[16,128,512]{2,1,0:T(8,128)S(1)} %fusion.44, s32[16]{0:T(128)S(1)} %get-tuple-element.118, pred[16]{0:T(512)(128)(4,1)S(1)} %add_compare_fusion.2), kind=kOutput, calls=%fused_computation.7.clone.1 | convolution fusion | flops 101187968 | bytes 8388688 | tf_op jit(solution)/shard_map/while/body/kc,kjf->cjf/dot_general | solution.py:55
  162.1 2.7 copy.25
  165.6 85.4 %all_to_all.16 = f32[32,16,512]{2,1,0:T(8,128)S(1)} all-to-all(f32[32,16,512]{2,1,0:T(8,128)S(1)} %bitcast.42), channel_id=1, replica_groups=mesh['dom'=32,'rep'=8] {'dom'}, dimensions={0} | all-to-all | bytes 2097152 | tf_op jit(solution)/shard_map/all_to_all | solution.py:32
  251.9 6.0 %all-to-all-start.2 = ((f32[8,1,1024]{2,1,0:T(1,128)}), f32[8,1,1024]{2,1,0:T(1,128)S(1)}, u32[]{:S(2)}, u32[]{:S(2)}) async-start(f32[8,1,1024]{2,1,0:T(1,128)} %reshape.55), calls=%async_computation.2 | async-start | bytes 65536 | tf_op jit(solution)/shard_map/all_to_all | solution.py:32
  257.9 2.7 %convolution_convert_fusion = bf16[1024,512]{1,0:T(8,128)(2,1)} fusion(bf16[1024,512]{1,0:T(8,128)(2,1)S(1)} %bitcast.41, bf16[512,512]{1,0:T(8,128)(2,1)} %param.11), kind=kOutput, calls=%fused_computation.30 | convolution fusion | flops 537395200 | bytes 2621440 | tf_op jit(solution)/shard_map/dot_general | solution.py:87
  260.7 2.0 all-to-all-done.2
  (36 shorter events, 6.9 us)
Async XLA Ops:
  7.2 157.7 %copy-start = (bf16[1024,512]{1,0:T(8,128)(2,1)S(1)}, bf16[1024,512]{1,0:T(8,128)(2,1)}, u32[]{:S(2)}) copy-start(bf16[1024,512]{1,0:T(8,128)(2,1)} %param.10) | copy-start | bytes 3145732
  7.2 101.5 %all-gather.2.cloned.1.call-start = ((), (), s32[]{:S(2)}) async-start(), calls=%async_computation.3 | async-start | bytes 9437184 | tf_op jit(solution)/shard_map/all_gather | solution.py:82
  61.1 49.2 %copy-start.1 = (s32[128,2]{0,1:T(2,128)S(1)}, s32[128,2]{0,1:T(2,128)}, u32[]{:S(2)}) copy-start(s32[128,2]{0,1:T(2,128)} %param.13) | copy-start | bytes 3076
  251.9 10.8 %all-to-all-start.2 = ((f32[8,1,1024]{2,1,0:T(1,128)}), f32[8,1,1024]{2,1,0:T(1,128)S(1)}, u32[]{:S(2)}, u32[]{:S(2)}) async-start(f32[8,1,1024]{2,1,0:T(1,128)} %reshape.55), calls=%async_computation.2 | async-start | bytes 65536 | tf_op jit(solution)/shard_map/all_to_all | solution.py:32
Sparse Core Ops, SparseCore 0:
  61.2 47.3 all-gather.1
where the time goes:
time: 273 us; the launch traced here: 271 us
  blocking collectives  131 us (48%)
  waiting for transfers between devices  48.9 us (18%)
  matrix products  35.9 us (13%)
  local copies, waits for them, and re-layouts  29.5 us (11%)
  between operations  14.8 us (5%)
  starting transfers between devices  6.07 us (2%)
  other arithmetic  4.88 us (2%)
    all_to_all x1, blocking collectives, sent_and_summed(): lax.all_to_all(parts, axis, split_axis=0, concat_axis=0, tiled=True)  85.4 us
    all_gather x1, waiting for transfers between devices, on_device(): whole = lax.all_gather(local_rows, 'rep', axis=0, tiled=True)  46.9 us
    all_to_all x1, blocking collectives, one_exchange(): parts = lax.all_to_all(parts, axis, split_axis=0, concat_axis=0, tiled=True)  45.9 us
    dot_general x4, matrix products, add_group(): jnp.einsum('kc,kjf->cjf', onehot, products, precision=lax.Precision.HIGHE...  25.1 us
    gather x4, local copies, waits for them, and re-layouts, add_group(): source = jnp.take(stacked, index_part[:, 0], axis=0)  16.2 us
    dot_general x4, matrix products, add_group(): jnp.einsum('kij,kif->kjf', block_part, source, preferred_element_type=jnp...  7.32 us
    all_to_all x1, starting transfers between devices, sent_and_summed(): lax.all_to_all(parts, axis, split_axis=0, concat_axis=0, tiled=True)  6.03 us
    scatter x1, local copies, waits for them, and re-layouts, on_device(): ordered = jnp.zeros_like(grad_out).at[target_slot].set(grad_out)  5.84 us
  transfers between devices with their start and end apart: 2, of which 2 were waited for; matrix products, arithmetic and copies ran while one was open for 1% of the time, Pallas kernels for 0%

commit v1 on v0

--- a/solution.py
+++ b/solution.py
@@ -79,7 +79,12 @@
     ordered = ordered.reshape(dom_count, rep_count, slot_rows, feat_width)
     arrived = one_exchange(ordered, ("dom", "rep"), ("dom", "rep"), (0, 1), (0, 1))
     local_rows = arrived.reshape(row_count, feat_width)
-    whole = lax.all_gather(local_rows, "rep", axis=0, tiled=True)
+    whole = jnp.concatenate(
+        jax.lax.all_to_all(
+            jnp.stack([local_rows for _ in range(jax.lax.axis_size("rep"))]), "rep", 0, 0
+        ),
+        0,
+    )
     stacked = whole.reshape(-1, block_side, feat_width)
     running = jnp.zeros((col_blocks, block_side, feat_width), jnp.float32)
     running = accumulate(running, edge_blocks, block_index, block_count[0], stacked)

time: 273 us -> 312 us (1.14)
  waiting for transfers between devices: 48.9 us -> 95 us
  between operations: 14.8 us -> 1.39 us
  starting transfers between devices: 6.07 us -> 12.2 us
    all_to_all x0 -> x1, waiting for transfers between devices: none -> 93.1 us  [on_device(): jax.lax.all_to_all(jnp.stack([local_rows for _ in range(jax.lax.axis_size...]
    all_gather x1 -> x0, waiting for transfers between devices: 46.9 us -> none  [on_device(): whole = lax.all_gather(local_rows, 'rep', axis=0, tiled=True)]
    all_to_all x0 -> x1, starting transfers between devices: none -> 6.33 us  [on_device(): jax.lax.all_to_all(jnp.stack([local_rows for _ in range(jax.lax.axis_size...]
    all_to_all x1, blocking collectives: 85.4 us -> 82.1 us  [sent_and_summed(): lax.all_to_all(parts, axis, split_axis=0, concat_axis=0, tiled=True)]
where the time goes in v1:
time: 312 us; the launch traced here: 310 us
  blocking collectives  128 us (41%)
  waiting for transfers between devices  95 us (30%)
  matrix products  36 us (12%)
  local copies, waits for them, and re-layouts  32.6 us (10%)
  starting transfers between devices  12.2 us (4%)
  other arithmetic  4.89 us (2%)
    all_to_all x1, waiting for transfers between devices, on_device(): jax.lax.all_to_all(jnp.stack([local_rows for _ in range(jax.lax.axis_size...  93.1 us
    all_to_all x1, blocking collectives, sent_and_summed(): lax.all_to_all(parts, axis, split_axis=0, concat_axis=0, tiled=True)  82.1 us
    all_to_all x1, blocking collectives, one_exchange(): parts = lax.all_to_all(parts, axis, split_axis=0, concat_axis=0, tiled=True)  45.9 us
    dot_general x4, matrix products, add_group(): jnp.einsum('kc,kjf->cjf', onehot, products, precision=lax.Precision.HIGHE...  25.1 us
    gather x4, local copies, waits for them, and re-layouts, add_group(): source = jnp.take(stacked, index_part[:, 0], axis=0)  16.2 us
    dot_general x4, matrix products, add_group(): jnp.einsum('kij,kif->kjf', block_part, source, preferred_element_type=jnp...  7.32 us
    all_to_all x1, starting transfers between devices, on_device(): jax.lax.all_to_all(jnp.stack([local_rows for _ in range(jax.lax.axis_size...  6.33 us
  transfers between devices with their start and end apart: 2, of which 2 were waited for; matrix products, arithmetic and copies ran while one was open for 1% of the time, Pallas kernels for 0%

profile of v1, /device:TPU:1, one launch (start us, length us, event | category | flops | bytes accessed | tf_op | source)
XLA Modules:
  0.0 310.2 jit_solution(10368401668536445255)
XLA Ops:
  1.4 5.8 %scatter_custom_fusion = bf16[1024,512]{1,0:T(8,128)(2,1)S(1)} fusion(s32[1024]{0:T(1024)S(1)} %compare_select_fusion.1, bf16[1024,512]{1,0:T(8,128)(2,1)} %param.9, bf16[]{:T(256)} %constant.78.clone.1), kind=kCustom, calls=%fused_computation.32 | custom fusion | bytes 1049088 | tf_op jit(solution)/shard_map/scatter | solution.py:78
  7.6 45.9 %all_to_all.20 = bf16[256,1,1,4,512]{4,3,2,1,0:T(4,128)(2,1)S(1)} all-to-all(bf16[256,1,1,4,512]{4,3,2,1,0:T(4,128)(2,1)S(1)} %bitcast.37), channel_id=1, replica_groups=mesh['dom'=32,'rep'=8] {'dom','rep'}, dimensions={0} | all-to-all | bytes 2097152 | tf_op jit(solution)/shard_map/all_to_all | solution.py:25
  53.7 3.9 %stack.3 = bf16[8,1024,512]{2,1,0:T(8,128)(2,1)} broadcast(bf16[1024,512]{1,0:T(8,128)(2,1)S(1)} %stack_reshape_reshape.2), dimensions={1,2} | broadcast | bytes 9437184 | tf_op jit(solution)/shard_map/stack | solution.py:84
  57.6 6.3 %all-to-all-start.1 = ((bf16[8,1024,512]{2,1,0:T(8,128)(2,1)}), bf16[8,1024,512]{2,1,0:T(8,128)(2,1)}, u32[]{:S(2)}, u32[]{:S(2)}) async-start(bf16[8,1024,512]{2,1,0:T(8,128)(2,1)} %stack.3), calls=%async_computation.1 | async-start | bytes 16777216 | tf_op jit(solution)/shard_map/all_to_all | solution.py:83
  64.7 93.1 %all-to-all-done.1 = bf16[8,1024,512]{2,1,0:T(8,128)(2,1)} async-done(((bf16[8,1024,512]{2,1,0:T(8,128)(2,1)}), bf16[8,1024,512]{2,1,0:T(8,128)(2,1)}, u32[]{:S(2)}, u32[]{:S(2)}) %all-to-all-start.1) | async-done | bytes 8388640 | tf_op jit(solution)/shard_map/all_to_all | solution.py:83
  157.7 1.7 broadcast_in_dim.29
  159.4 51.8 %while.10 = (s32[]{:T(128)}, f32[8,128,512]{2,0,1:T(8,128)}, s32[]{:T(128)}, s32[]{:T(128)}, s32[128,2]{0,1:T(2,128)S(1)}, /*index=5*/bf16[128,128,128]{2,1,0:T(...) while((s32[]{:T(128)}, f32[8,128,512]{2,0,1:T(8,128)}, ...), condition=%wide.region_2.3_spmd, body=%wide.region_1.2_spmd.sunk | while | flops 370673216 | bytes 19403756 | solution.py:63
  159.5 4.1 %gather_fusion = bf16[16,128,512]{2,1,0:T(8,128)(2,1)S(1)} fusion(bf16[64,128,512]{2,1,0:T(8,128)(2,1)} %get-tuple-element.147, s32[1024]{0:T(1024)S(1)} %pad_clamp_fusion.2), kind=kCustom, calls=%fused_computation.clone.1 | custom fusion | bytes 4194368 | tf_op jit(solution)/shard_map/while/body/jit(_take)/gather | solution.py:45
  163.6 1.8 fusion.44
  166.1 6.3 %fusion.45 = f32[8,128,512]{2,0,1:T(8,128)} fusion(f32[8,128,512]{2,0,1:T(8,128)} %get-tuple-element.131, f32[16,128,512]{2,1,0:T(8,128)S(1)} %fusion.44, s32[16]{0:T(128)S(1)} %get-tuple-element.118, pred[16]{0:T(512)(128)(4,1)S(1)} %add_compare_fusion.2), kind=kOutput, calls=%fused_computation.7.clone.1 | convolution fusion | flops 101187968 | bytes 8388688 | tf_op jit(solution)/shard_map/while/body/kc,kjf->cjf/dot_general | solution.py:55
  172.4 4.1 %gather_fusion = bf16[16,128,512]{2,1,0:T(8,128)(2,1)S(1)} fusion(bf16[64,128,512]{2,1,0:T(8,128)(2,1)} %get-tuple-element.147, s32[1024]{0:T(1024)S(1)} %pad_clamp_fusion.2), kind=kCustom, calls=%fused_computation.clone.1 | custom fusion | bytes 4194368 | tf_op jit(solution)/shard_map/while/body/jit(_take)/gather | solution.py:45
  176.5 1.8 fusion.44
  179.0 6.3 %fusion.45 = f32[8,128,512]{2,0,1:T(8,128)} fusion(f32[8,128,512]{2,0,1:T(8,128)} %get-tuple-element.131, f32[16,128,512]{2,1,0:T(8,128)S(1)} %fusion.44, s32[16]{0:T(128)S(1)} %get-tuple-element.118, pred[16]{0:T(512)(128)(4,1)S(1)} %add_compare_fusion.2), kind=kOutput, calls=%fused_computation.7.clone.1 | convolution fusion | flops 101187968 | bytes 8388688 | tf_op jit(solution)/shard_map/while/body/kc,kjf->cjf/dot_general | solution.py:55
  185.4 4.1 %gather_fusion = bf16[16,128,512]{2,1,0:T(8,128)(2,1)S(1)} fusion(bf16[64,128,512]{2,1,0:T(8,128)(2,1)} %get-tuple-element.147, s32[1024]{0:T(1024)S(1)} %pad_clamp_fusion.2), kind=kCustom, calls=%fused_computation.clone.1 | custom fusion | bytes 4194368 | tf_op jit(solution)/shard_map/while/body/jit(_take)/gather | solution.py:45
  189.4 1.8 fusion.44
  191.9 6.3 %fusion.45 = f32[8,128,512]{2,0,1:T(8,128)} fusion(f32[8,128,512]{2,0,1:T(8,128)} %get-tuple-element.131, f32[16,128,512]{2,1,0:T(8,128)S(1)} %fusion.44, s32[16]{0:T(128)S(1)} %get-tuple-element.118, pred[16]{0:T(512)(128)(4,1)S(1)} %add_compare_fusion.2), kind=kOutput, calls=%fused_computation.7.clone.1 | convolution fusion | flops 101187968 | bytes 8388688 | tf_op jit(solution)/shard_map/while/body/kc,kjf->cjf/dot_general | solution.py:55
  198.3 4.1 %gather_fusion = bf16[16,128,512]{2,1,0:T(8,128)(2,1)S(1)} fusion(bf16[64,128,512]{2,1,0:T(8,128)(2,1)} %get-tuple-element.147, s32[1024]{0:T(1024)S(1)} %pad_clamp_fusion.2), kind=kCustom, calls=%fused_computation.clone.1 | custom fusion | bytes 4194368 | tf_op jit(solution)/shard_map/while/body/jit(_take)/gather | solution.py:45
  202.4 1.8 fusion.44
  204.9 6.3 %fusion.45 = f32[8,128,512]{2,0,1:T(8,128)} fusion(f32[8,128,512]{2,0,1:T(8,128)} %get-tuple-element.131, f32[16,128,512]{2,1,0:T(8,128)S(1)} %fusion.44, s32[16]{0:T(128)S(1)} %get-tuple-element.118, pred[16]{0:T(512)(128)(4,1)S(1)} %add_compare_fusion.2), kind=kOutput, calls=%fused_computation.7.clone.1 | convolution fusion | flops 101187968 | bytes 8388688 | tf_op jit(solution)/shard_map/while/body/kc,kjf->cjf/dot_general | solution.py:55
  211.2 2.7 copy.25
  214.7 82.1 %all_to_all.21 = f32[32,16,512]{2,1,0:T(8,128)S(1)} all-to-all(f32[32,16,512]{2,1,0:T(8,128)S(1)} %bitcast.41), channel_id=1, replica_groups=mesh['dom'=32,'rep'=8] {'dom'}, dimensions={0} | all-to-all | bytes 2097152 | tf_op jit(solution)/shard_map/all_to_all | solution.py:32
  297.7 5.9 %all-to-all-start.3 = ((f32[8,1,1024]{2,1,0:T(1,128)}), f32[8,1,1024]{2,1,0:T(1,128)S(1)}, u32[]{:S(2)}, u32[]{:S(2)}) async-start(f32[8,1,1024]{2,1,0:T(1,128)} %reshape.53), calls=%async_computation.3 | async-start | bytes 65536 | tf_op jit(solution)/shard_map/all_to_all | solution.py:32
  303.6 2.8 convolution_convert_fusion
  306.3 2.0 all-to-all-done.3
  (36 shorter events, 7.9 us)
Async XLA Ops:
  0.6 213.3 %copy-start = (bf16[1024,512]{1,0:T(8,128)(2,1)S(1)}, bf16[1024,512]{1,0:T(8,128)(2,1)}, u32[]{:S(2)}) copy-start(bf16[1024,512]{1,0:T(8,128)(2,1)} %param.10) | copy-start | bytes 3145732
  57.6 100.1 %all-to-all-start.1 = ((bf16[8,1024,512]{2,1,0:T(8,128)(2,1)}), bf16[8,1024,512]{2,1,0:T(8,128)(2,1)}, u32[]{:S(2)}, u32[]{:S(2)}) async-start(bf16[8,1024,512]{2,1,0:T(8,128)(2,1)} %stack.3), calls=%async_computation.1 | async-start | bytes 16777216 | tf_op jit(solution)/shard_map/all_to_all | solution.py:83
  64.0 95.4 %copy-start.1 = (s32[128,2]{0,1:T(2,128)S(1)}, s32[128,2]{0,1:T(2,128)}, u32[]{:S(2)}) copy-start(s32[128,2]{0,1:T(2,128)} %param.13) | copy-start | bytes 3076
  297.7 10.6 %all-to-all-start.3 = ((f32[8,1,1024]{2,1,0:T(1,128)}), f32[8,1,1024]{2,1,0:T(1,128)S(1)}, u32[]{:S(2)}, u32[]{:S(2)}) async-start(f32[8,1,1024]{2,1,0:T(1,128)} %reshape.53), calls=%async_computation.3 | async-start | bytes 65536 | tf_op jit(solution)/shard_map/all_to_all | solution.py:32
